TPU v7x, 512 devices: a whole 4x4x16 slice. The times are simulated.
512 devices in a mesh: dp: 4 (over x), ctx: 32 (over z, core), tp: 4 (over y).
Axes of the slice: x: 4, y: 4, z: 16, core: 2. Of those that a mesh axis runs over, the one named last changes fastest.
Arguments:
- inputs: bfloat16 [4, 4096, 8192], P('dp', 'ctx', 'tp'), may hold values from -6 to 6
- grad_out: bfloat16 [4, 4096, 8192], P('dp', 'ctx', 'tp'), may hold values from -6 to 6
- input_map: bfloat16 [4, 4096, 128], P('dp', 'ctx'), may hold values from -0.5 to 0.5
- output_map: bfloat16 [4, 4096, 128], P('dp', 'ctx'), may hold values from -0.25 to 0.25
- step_size: float32 [4, 128, 4096], P('dp', 'tp', 'ctx'), may hold values from 0.3 to 1.5
- log_decay: float32 [4, 128, 4096], P('dp', 'tp', 'ctx'), may hold values from -2 to 0
- skip_gain: float32 [128], P('tp'), may hold values from 0.5 to 1.5
Outputs:
- mixed: bfloat16 [4, 4096, 8192], P('dp', 'ctx', 'tp')
- grad_inputs: bfloat16 [4, 4096, 8192], P('dp', 'ctx', 'tp')
- grad_step: float32 [4, 128, 4096], P('dp', 'tp', 'ctx')
- grad_decay: float32 [4, 128, 4096], P('dp', 'tp', 'ctx')
- grad_input_map: float32 [4, 4096, 128], P('dp', ('ctx', 'tp'))
- grad_output_map: float32 [4, 4096, 128], P('dp', ('ctx', 'tp'))
- grad_skip: float32 [128], P('tp')
All inputs are finite; a program needn't handle non-finite values.
Results may differ from a plain program's by a relative error of at most 0.0011.
Values sent between devices are 32-bit elements; how exact they have to be, the bound alone decides.
No kernel may reach another device: no remote copies, remote signals or barrier semaphores. Data moves between devices by JAX's collectives and lax.ppermute only.
A program may use at most 192 MiB of HBM per device.

v0:
```python
import math
import jax
import jax.numpy as jnp
from jax import lax
from jax.sharding import PartitionSpec as P

precise = lax.Precision.HIGHEST


def entering(part, axis, combine, identity, reverse):
    count = lax.axis_size(axis)
    place = lax.axis_index(axis)
    ahead = count - 1 - place if reverse else place
    gathered = jax.tree.map(lambda a: lax.all_gather(a, axis), part)
    state = jax.tree.map(lambda a, e: jnp.zeros_like(a) + jnp.asarray(e, a.dtype), part, identity)

    def one(hop, state):
        source = count - 1 - hop if reverse else hop
        return combine(
            state, jax.tree.map(lambda a: lax.dynamic_index_in_dim(a, source, 0, False), gathered)
        )

    return lax.fori_loop(0, ahead, one, state)


def combine_pair(earlier, later_part):
    return (earlier[0] * later_part[0], later_part[0][..., None, None] * earlier[1] + later_part[1])


def block_forward(values, in_map, out_map, steps, logs):
    cumulative = jnp.cumsum(logs, axis=-1)
    length = cumulative.shape[-1]
    row_ids = lax.broadcasted_iota(jnp.int32, (length, length), 0)
    column_ids = lax.broadcasted_iota(jnp.int32, (length, length), 1)
    causal = row_ids >= column_ids
    spread = cumulative[..., :, None] - cumulative[..., None, :]
    decays = jnp.where(causal, jnp.exp(jnp.where(causal, spread, 0.0)), 0.0)
    affinity = jnp.einsum("btn,bsn->bts", out_map, in_map, precision=precise)
    mixing = decays * affinity[:, None]
    scaled = values * jnp.transpose(steps, (0, 2, 1))[..., None]
    remain = jnp.exp(cumulative[..., -1:] - cumulative)
    weighted = remain[..., None] * in_map[:, None]
    local_state = jnp.einsum("bshp,bhsn->bhpn", scaled, weighted, precision=precise)
    through = jnp.exp(cumulative[..., -1])
    return (cumulative, decays, mixing, scaled, remain, local_state, through)


def block_output(values, out_map, skip_gain, cumulative, mixing, scaled, incoming):
    within = jnp.einsum("bhts,bshp->bthp", mixing, scaled, precision=precise)
    carried = jnp.einsum("bhpn,btn->bthp", incoming, out_map, precision=precise)
    carried = carried * jnp.transpose(jnp.exp(cumulative), (0, 2, 1))[..., None]
    return (within + carried + skip_gain[:, None] * values, carried)


def block_source(cotangent, out_map, cumulative):
    weighted = jnp.exp(cumulative)[..., None] * out_map[:, None]
    return jnp.einsum("bshp,bhsn->bhpn", cotangent, weighted, precision=precise)


def block_backward(
    values,
    cotangent,
    in_map,
    out_map,
    steps,
    skip_gain,
    cumulative,
    decays,
    mixing,
    scaled,
    remain,
    local_state,
    through,
    incoming,
    carried,
    arriving,
):
    remain_col = jnp.transpose(remain, (0, 2, 1))[..., None]
    starts = jnp.transpose(jnp.exp(cumulative), (0, 2, 1))[..., None]
    steps_col = jnp.transpose(steps, (0, 2, 1))[..., None]
    from_later = jnp.einsum("bhpn,btn->bthp", arriving, in_map, precision=precise)
    state_grad = (
        jnp.einsum("bhst,bshp->bthp", mixing, cotangent, precision=precise)
        + remain_col * from_later
    )
    grad_values = steps_col * state_grad + skip_gain[:, None] * cotangent
    grad_steps = jnp.transpose(jnp.sum(values * state_grad, axis=-1), (0, 2, 1))
    products = jnp.einsum("bthp,bshp->bhts", cotangent, scaled, precision=precise)
    summed = jnp.sum(decays * products, axis=1)
    grad_in_map = jnp.einsum("bts,btn->bsn", summed, out_map, precision=precise) + jnp.einsum(
        "bthp,bhpn->btn", scaled * remain_col, arriving, precision=precise
    )
    grad_out_map = jnp.einsum("bts,bsn->btn", summed, in_map, precision=precise) + jnp.einsum(
        "bthp,bhpn->btn", cotangent * starts, incoming, precision=precise
    )
    paired = mixing * products
    change = jnp.sum(paired, axis=-1) - jnp.sum(paired, axis=-2)
    change = change + jnp.transpose(jnp.sum(cotangent * carried, axis=-1), (0, 2, 1))
    change = change - remain * jnp.transpose(jnp.sum(scaled * from_later, axis=-1), (0, 2, 1))
    final_edge = jnp.sum(arriving * local_state, axis=(2, 3)) + through * jnp.sum(
        arriving * incoming, axis=(2, 3)
    )
    length = change.shape[-1]
    ending = lax.broadcasted_iota(jnp.int32, (length,), 0) == length - 1
    change = change + jnp.where(ending, final_edge[..., None], 0.0)
    grad_logs = lax.cumsum(change, axis=2, reverse=True)
    skip_part = jnp.sum(cotangent * values, axis=(0, 1, 3))
    return (grad_values, grad_steps, grad_in_map, grad_out_map, grad_logs, skip_part)


def shards(inputs, grad_out, input_map, output_map, step_size, log_decay, skip_gain):
    sequences, length, features = inputs.shape
    heads = step_size.shape[1]
    per_head = features // heads
    values = inputs.reshape(sequences, length, heads, per_head).astype(jnp.float32)
    cotangent = grad_out.reshape(sequences, length, heads, per_head).astype(jnp.float32)
    in_map = input_map.astype(jnp.float32)
    out_map = output_map.astype(jnp.float32)
    cumulative, decays, mixing, scaled, remain, local_state, through = block_forward(
        values, in_map, out_map, step_size, log_decay
    )
    source = block_source(cotangent, out_map, cumulative)
    neutral = (jnp.ones_like(through), jnp.zeros_like(local_state))
    ahead = entering((through, local_state), "ctx", combine_pair, neutral, False)
    behind = entering((through, source), "ctx", combine_pair, neutral, True)
    incoming = ahead[1]
    arriving = behind[1]
    mixed, carried = block_output(values, out_map, skip_gain, cumulative, mixing, scaled, incoming)
    results = block_backward(
        values,
        cotangent,
        in_map,
        out_map,
        step_size,
        skip_gain,
        cumulative,
        decays,
        mixing,
        scaled,
        remain,
        local_state,
        through,
        incoming,
        carried,
        arriving,
    )
    grad_values, grad_steps, grad_in_part, grad_out_part, grad_logs, skip_part = results
    grad_in_map, grad_out_map = (
        lax.psum_scatter(grad_in_part, "tp", scatter_dimension=1, tiled=True),
        lax.psum_scatter(grad_out_part, "tp", scatter_dimension=1, tiled=True),
    )
    skip_total = lax.psum(skip_part, ("dp", "ctx"))
    factor = 1.0 / math.sqrt(
        sequences * lax.axis_size("dp") * length * lax.axis_size("ctx") * per_head
    )
    mixed_out = mixed.reshape(sequences, length, features).astype(jnp.bfloat16)
    grad_inputs = grad_values.reshape(sequences, length, features).astype(jnp.bfloat16)
    return (
        mixed_out,
        grad_inputs,
        grad_steps,
        grad_logs,
        grad_in_map,
        grad_out_map,
        skip_total * factor,
    )


def solution(mesh):
    in_specs = (
        P("dp", "ctx", "tp"),
        P("dp", "ctx", "tp"),
        P("dp", "ctx", None),
        P("dp", "ctx", None),
        P("dp", "tp", "ctx"),
        P("dp", "tp", "ctx"),
        P("tp"),
    )
    out_specs = (
        P("dp", "ctx", "tp"),
        P("dp", "ctx", "tp"),
        P("dp", "tp", "ctx"),
        P("dp", "tp", "ctx"),
        P("dp", ("ctx", "tp"), None),
        P("dp", ("ctx", "tp"), None),
        P("tp"),
    )
    return jax.shard_map(shards, mesh=mesh, in_specs=in_specs, out_specs=out_specs, check_vma=False)
```

profile of v0, /device:TPU:2, one launch (start us, length us, event | category | flops | bytes accessed | tf_op | source)
XLA Modules:
  0.0 737.4 jit_solution(14283848565593800011)
XLA Ops:
  9.9 3.2 fusion.3
  13.5 2.4 fusion.16
  16.1 36.1 %all-gather = f32[32,32,1]{1,2,0:T(1,128)S(1)} all-gather(f32[1,32,1]{1,2,0:T(1,128)S(1)} %exp.61), channel_id=2, replica_groups=mesh['dp'=4,'ctx'=32,'tp'=4] {'ctx'}, dimensions={0}, use_global_device_ids=true | all-gather | bytes 4224 | tf_op jit(solution)/shard_map/all_gather | solution.py:14
  52.3 3.1 fusion.20
  55.4 153.7 %all-gather.6.cloned.1.call-done = f32[1024,64,128]{2,1,0:T(8,128)} async-done(((f32[32,64,128]{2,1,0:T(8,128)}), f32[1024,64,128]{2,1,0:T(8,128)}) %all-gather.6.cloned.1.call-update) | async-done | bytes 33554448 | tf_op jit(solution)/shard_map/all_gather | solution.py:14
  209.2 191.1 %all-gather.8.cloned.1.call-done = f32[1024,64,128]{2,1,0:T(8,128)} async-done(((f32[32,64,128]{2,1,0:T(8,128)}), f32[1024,64,128]{2,1,0:T(8,128)}) %all-gather.8.cloned.1.call-update) | async-done | bytes 33554448 | tf_op jit(solution)/shard_map/all_gather | solution.py:14
  400.4 46.3 %while.27 = (s32[]{:T(128)}, f32[1,32,64,128]{3,2,1,0:T(8,128)S(1)}, s32[]{:T(128)}, f32[32,1,32]{2,1,0:T(1,128)S(1)}, f32[32,1,32,64,128]{4,3,2,1,0:T(8,128)}, ...) while((s32[]{:T(128)}, f32[1,32,64,128]{3,2,1,0:T(8,128)S(1)}, s32[]{:T(128)}, f32[32,1,32]{2,1,0:T(1,128)S(1)}, ...), condition=%wide.region_4.5_spmd, body=%wide.region_3.4_spmd.sunk | while | flops 524294 | bytes 3146259 | solution.py:23
  400.4 1.4 bitcast_add_fusion.6
  401.9 1.4 bitcast_add_fusion.6
  403.4 1.4 bitcast_add_fusion.6
  404.9 1.4 bitcast_add_fusion.6
  406.4 1.4 bitcast_add_fusion.6
  415.4 1.4 bitcast_add_fusion.6
  434.8 1.4 bitcast_add_fusion.6
  443.8 1.4 bitcast_add_fusion.6
  446.7 1.6 multiply_reduce_fusion.2
  449.4 1.6 multiply_reduce_fusion.3
  452.4 1.9 convolution_bitcast_fusion.2
  455.5 3.8 fusion.31
  459.3 3.2 multiply_reduce_fusion.4
  462.4 1.9 convolution_bitcast_fusion.3
  466.5 208.1 %psum.7 = f32[32]{0:T(128)S(1)} all-reduce(f32[32]{0:T(128)S(1)} %reduce_sum.113), channel_id=1, replica_groups=mesh['dp'=4,'ctx'=32,'tp'=4] {'dp','ctx'}, use_global_device_ids=true, to_apply=%region_18.19 | all-reduce | flops 32 | bytes 256 | tf_op jit(solution)/shard_map/psum | solution.py:152
  675.4 1.8 reduce_window_sum.22
  677.8 53.1 %reduce-scatter.3.cloned.1.call-done = f32[1,32,128]{2,1,0:T(8,128)} async-done(((f32[1,128,128]{2,1,0:T(8,128)}), f32[1,32,128]{2,1,0:T(8,128)}) %reduce-scatter.3.cloned.1.call-update) | async-done | bytes 16400 | tf_op jit(solution)/shard_map/reduce_scatter | solution.py:149
  (117 shorter events, 44.1 us)
Async XLA Ops:
  7.2 2.7 copy-start.8
  7.2 2.8 copy-start.11
  7.2 201.8 %all-gather.6.cloned.1.call-start = ((), (), s32[]{:S(2)}) async-start(), calls=%async_computation.4 | async-start | bytes 34603008 | tf_op jit(solution)/shard_map/all_gather | solution.py:14
  9.8 3.3 copy-start.4
  9.8 3.4 copy-start.10
  9.9 3.6 copy-start.9
  13.1 387.1 %all-gather.8.cloned.1.call-start = ((), (), s32[]{:S(2)}) async-start(), calls=%async_computation.5 | async-start | bytes 34603008 | tf_op jit(solution)/shard_map/all_gather | solution.py:14
  13.5 41.9 %copy-start.1 = (bf16[1,128,2048]{1,2,0:T(8,128)(2,1)}, bf16[1,128,2048]{1,2,0:T(8,128)(2,1)S(1)}, u32[]{:S(2)}) copy-start(bf16[1,128,2048]{1,2,0:T(8,128)(2,1)S(1)} %copy.84) | copy-start | bytes 1572868
  16.0 661.8 %reduce-scatter.5.cloned.1.call-start = ((), (), s32[]{:S(2)}) async-start(), calls=%async_computation.3 | async-start | bytes 81920 | tf_op jit(solution)/shard_map/reduce_scatter | solution.py:150
  446.7 1.6 copy-start
  448.3 1.0 copy-start.2
  449.4 1.7 copy-start.5
  451.1 4.3 copy-start.12
  455.2 275.7 %reduce-scatter.3.cloned.1.call-start = ((), (), s32[]{:S(2)}) async-start(), calls=%async_computation.2 | async-start | bytes 81920 | tf_op jit(solution)/shard_map/reduce_scatter | solution.py:149
  455.4 3.8 copy-start.3
  455.5 3.8 copy-start.7
  459.3 3.2 copy-start.6
Sparse Core Ops, SparseCore 0:
  13.3 195.7 all-gather.5
  211.1 189.0 all-gather.7
  455.3 18.9 reduce-scatter.4
  675.5 55.2 reduce-scatter.2
where the time goes:
time: 739 us; the launch traced here: 737 us
  waiting for transfers between devices  398 us (54%)
  blocking collectives  244 us (33%)
  other arithmetic  50.2 us (7%)
  matrix products  24.4 us (3%)
  between operations  14.1 us (2%)
    all_gather x2, waiting for transfers between devices, entering(): gathered = jax.tree.map(lambda a: lax.all_gather(a, axis), part)  345 us
    psum x1, blocking collectives, shards(): skip_total = lax.psum(skip_part, ('dp', 'ctx'))  208 us
    reduce_scatter x1, waiting for transfers between devices, shards(): lax.psum_scatter(grad_in_part, 'tp', scatter_dimension=1, tiled=True)  53.1 us
    add x31, other arithmetic, combine_pair(): later_part[0][..., None, None] * earlier[1] + later_part[1]  44.9 us
    all_gather x1, blocking collectives, entering(): gathered = jax.tree.map(lambda a: lax.all_gather(a, axis), part)  36.1 us
  transfers between devices with their start and end apart: 4, of which 3 were waited for; matrix products, arithmetic and copies ran while one was open for 3% of the time, Pallas kernels for 0%

commit v1 on v0

--- a/solution.py
+++ b/solution.py
@@ -5,6 +5,12 @@
 from jax.sharding import PartitionSpec as P
 
 precise = lax.Precision.HIGHEST
+
+
+def gather_and_add(value, mesh_axis):
+    terms = lax.all_gather(value, mesh_axis, axis=0, tiled=False)
+    summed = terms.sum(axis=0)
+    return summed
 
 
 def entering(part, axis, combine, identity, reverse):
@@ -149,7 +155,7 @@
         lax.psum_scatter(grad_in_part, "tp", scatter_dimension=1, tiled=True),
         lax.psum_scatter(grad_out_part, "tp", scatter_dimension=1, tiled=True),
     )
-    skip_total = lax.psum(skip_part, ("dp", "ctx"))
+    skip_total = gather_and_add(skip_part, ("dp", "ctx"))
     factor = 1.0 / math.sqrt(
         sequences * lax.axis_size("dp") * length * lax.axis_size("ctx") * per_head
     )

time: 739 us -> 985 us (1.33)
  blocking collectives: 244 us -> 456 us
  waiting for transfers between devices: 398 us -> 428 us
    unnamed x0 -> x1, blocking collectives: none -> 420 us
    psum x1 -> x0, blocking collectives: 208 us -> none  [shards(): skip_total = lax.psum(skip_part, ('dp', 'ctx'))]
    reduce_scatter x1, waiting for transfers between devices: 53.1 us -> 85 us  [shards(): lax.psum_scatter(grad_in_part, 'tp', scatter_dimension=1, tiled=True)]
  transfers between devices with their start and end apart: 4 -> 4, of which waited for: 3 -> 3; matrix products, arithmetic and copies ran while one was open for 3% -> 2% of each run, Pallas kernels for 0% -> 0%
where the time goes in v1:
time: 985 us; the launch traced here: 983 us
  blocking collectives  456 us (46%)
  waiting for transfers between devices  428 us (43%)
  other arithmetic  50.3 us (5%)
  matrix products  25.8 us (3%)
  between operations  14.7 us (1%)
    unnamed x1, blocking collectives  420 us
    all_gather x2, waiting for transfers between devices, entering(): gathered = jax.tree.map(lambda a: lax.all_gather(a, axis), part)  343 us
    reduce_scatter x1, waiting for transfers between devices, shards(): lax.psum_scatter(grad_in_part, 'tp', scatter_dimension=1, tiled=True)  85 us
    add x31, other arithmetic, combine_pair(): later_part[0][..., None, None] * earlier[1] + later_part[1]  44.9 us
    all_gather x1, blocking collectives, entering(): gathered = jax.tree.map(lambda a: lax.all_gather(a, axis), part)  36.1 us
  transfers between devices with their start and end apart: 4, of which 3 were waited for; matrix products, arithmetic and copies ran while one was open for 2% of the time, Pallas kernels for 0%

profile of v1, /device:TPU:2, one launch (start us, length us, event | category | flops | bytes accessed | tf_op | source)
XLA Modules:
  0.0 983.3 jit_solution(3786408761635333082)
XLA Ops:
  9.9 3.2 fusion.3
  13.5 2.4 fusion.16
  18.0 36.1 %all-gather = f32[32,32,1]{1,2,0:T(1,128)S(1)} all-gather(f32[1,32,1]{1,2,0:T(1,128)S(1)} %exp.61), channel_id=2, replica_groups=mesh['dp'=4,'ctx'=32,'tp'=4] {'ctx'}, dimensions={0}, use_global_device_ids=true | all-gather | bytes 4224 | tf_op jit(solution)/shard_map/all_gather | solution.py:20
  54.2 3.1 fusion.20
  57.3 151.7 %all-gather.7.cloned.1.call-done = f32[1024,64,128]{2,1,0:T(8,128)} async-done(((f32[32,64,128]{2,1,0:T(8,128)}), f32[1024,64,128]{2,1,0:T(8,128)}) %all-gather.7.cloned.1.call-update) | async-done | bytes 33554448 | tf_op jit(solution)/shard_map/all_gather | solution.py:20
  209.2 191.1 %all-gather.9.cloned.1.call-done = f32[1024,64,128]{2,1,0:T(8,128)} async-done(((f32[32,64,128]{2,1,0:T(8,128)}), f32[1024,64,128]{2,1,0:T(8,128)}) %all-gather.9.cloned.1.call-update) | async-done | bytes 33554448 | tf_op jit(solution)/shard_map/all_gather | solution.py:20
  400.4 46.3 %while.27 = (s32[]{:T(128)}, f32[1,32,64,128]{3,2,1,0:T(8,128)S(1)}, s32[]{:T(128)}, f32[32,1,32]{2,1,0:T(1,128)S(1)}, f32[32,1,32,64,128]{4,3,2,1,0:T(8,128)}, ...) while((s32[]{:T(128)}, f32[1,32,64,128]{3,2,1,0:T(8,128)S(1)}, s32[]{:T(128)}, f32[32,1,32]{2,1,0:T(1,128)S(1)}, ...), condition=%wide.region_4.5_spmd, body=%wide.region_3.4_spmd.sunk | while | flops 524294 | bytes 3146259 | solution.py:29
  400.4 1.4 bitcast_add_fusion.6
  401.9 1.4 bitcast_add_fusion.6
  403.4 1.4 bitcast_add_fusion.6
  404.9 1.4 bitcast_add_fusion.6
  407.9 1.4 bitcast_add_fusion.6
  416.9 1.4 bitcast_add_fusion.6
  436.3 1.4 bitcast_add_fusion.6
  445.3 1.4 bitcast_add_fusion.6
  446.7 1.6 multiply_reduce_fusion.2
  449.4 1.6 multiply_reduce_fusion.3
  452.4 1.9 convolution_bitcast_fusion.2
  455.5 4.6 fusion.31
  460.0 3.9 multiply_reduce_fusion.4
  463.9 1.8 convolution_bitcast_fusion.3
  466.2 420.2 %all-reduce = f32[4096]{0:T(1024)S(1)} all-reduce(f32[4096]{0:T(1024)S(1)} %dynamic-update-slice), channel_id=5, replica_groups=mesh['dp'=4,'ctx'=32,'tp'=4] {'dp','ctx'}, use_global_device_ids=true, to_apply=%add | all-reduce | flops 4096 | bytes 32768
  889.4 1.8 reduce_window_sum.22
  891.7 85.0 %reduce-scatter.3.cloned.1.call-done = f32[1,32,128]{2,1,0:T(8,128)} async-done(((f32[1,128,128]{2,1,0:T(8,128)}), f32[1,32,128]{2,1,0:T(8,128)}) %reduce-scatter.3.cloned.1.call-update) | async-done | bytes 16400 | tf_op jit(solution)/shard_map/reduce_scatter | solution.py:155
  (126 shorter events, 45.7 us)
Async XLA Ops:
  7.2 2.7 copy-start.8
  7.2 2.8 copy-start.13
  7.2 201.8 %all-gather.7.cloned.1.call-start = ((), (), s32[]{:S(2)}) async-start(), calls=%async_computation.4 | async-start | bytes 34603008 | tf_op jit(solution)/shard_map/all_gather | solution.py:20
  9.8 3.3 copy-start.4
  9.8 3.4 copy-start.10
  9.9 3.6 copy-start.9
  13.1 387.1 %all-gather.9.cloned.1.call-start = ((), (), s32[]{:S(2)}) async-start(), calls=%async_computation.5 | async-start | bytes 34603008 | tf_op jit(solution)/shard_map/all_gather | solution.py:20
  13.5 43.8 %copy-start.1 = (bf16[1,128,2048]{1,2,0:T(8,128)(2,1)}, bf16[1,128,2048]{1,2,0:T(8,128)(2,1)S(1)}, u32[]{:S(2)}) copy-start(bf16[1,128,2048]{1,2,0:T(8,128)(2,1)S(1)} %copy.84) | copy-start | bytes 1572868
  16.0 875.7 %reduce-scatter.5.cloned.1.call-start = ((), (), s32[]{:S(2)}) async-start(), calls=%async_computation.3 | async-start | bytes 81920 | tf_op jit(solution)/shard_map/reduce_scatter | solution.py:156
  446.7 1.6 copy-start
  448.3 1.0 copy-start.2
  449.4 1.7 copy-start.5
  451.1 4.3 copy-start.14
  455.2 521.5 %reduce-scatter.3.cloned.1.call-start = ((), (), s32[]{:S(2)}) async-start(), calls=%async_computation.2 | async-start | bytes 81920 | tf_op jit(solution)/shard_map/reduce_scatter | solution.py:155
  455.4 4.6 copy-start.3
  455.5 4.6 copy-start.7
  460.0 3.9 copy-start.6
  463.9 422.6 %copy-start.12 = (bf16[1,128,32,64]{1,3,2,0:T(8,128)(2,1)S(1)}, bf16[1,128,32,64]{1,3,2,0:T(8,128)(2,1)}, u32[]{:S(2)}) copy-start(bf16[1,128,32,64]{1,3,2,0:T(8,128)(2,1)} %get-tuple-element.248) | copy-start | bytes 1572868
  463.9 423.6 %copy-start.11 = (bf16[1,128,32,64]{1,3,2,0:T(8,128)(2,1)S(1)}, bf16[1,128,32,64]{1,3,2,0:T(8,128)(2,1)}, u32[]{:S(2)}) copy-start(bf16[1,128,32,64]{1,3,2,0:T(8,128)(2,1)} %fusion.31) | copy-start | bytes 1572868
Sparse Core Ops, SparseCore 0:
  13.3 195.7 all-gather.6
  211.1 189.0 all-gather.8
  455.3 19.0 reduce-scatter.4
  889.5 87.2 reduce-scatter.2
